TPU v7x, 128 devices: a whole 4x4x4 slice. The times are simulated.
128 devices in a mesh: shard: 16 (over x_lo, z, core), tensor: 4 (over y), section: 2 (over x_hi).
Axes of the slice: x: 4 (x_hi: 2, x_lo: 2; x = x_hi * 2 + x_lo), y: 4, z: 4, core: 2. Of those that a mesh axis runs over, the one named last changes fastest.
Arguments:
- grads: bfloat16 [2, 4, 16, 2048, 1536], P('section', 'tensor', 'shard'), may hold values from -12 to 12
- gain_grads: float32 [2, 64, 2048], P('section', ('shard', 'tensor')), may hold values from -614 to 614
- master: float32 [2, 4, 1536, 2048], P('section', 'tensor', 'shard'), may hold values from -0.12 to 0.12
- moment1: float32 [2, 4, 1536, 2048], P('section', 'tensor', 'shard'), may hold values from -0.6 to 0.6
- moment2: float32 [2, 4, 1536, 2048], P('section', 'tensor', 'shard'), may hold values from 0.005 to 0.5
- average: float32 [2, 4, 2048, 1536], P('section', 'tensor', 'shard'), may hold values from -0.12 to 0.12
- gain_master: float32 [2, 2048], P('section'), may hold values from 0.5 to 1.5
- gain_m: float32 [2, 2048], P('section'), may hold values from -30 to 30
- gain_v: float32 [2, 2048], P('section'), may hold values from 20 to 2000
Outputs:
- new_master: float32 [2, 4, 1536, 2048], P('section', 'tensor', 'shard')
- new_m: float32 [2, 4, 1536, 2048], P('section', 'tensor', 'shard')
- new_v: float32 [2, 4, 1536, 2048], P('section', 'tensor', 'shard')
- weights: bfloat16 [2, 4, 2048, 1536], P('section', 'tensor')
- new_average: float32 [2, 4, 2048, 1536], P('section', 'tensor', 'shard')
- new_gain: float32 [2, 2048], P('section')
- new_gain_m: float32 [2, 2048], P('section')
- new_gain_v: float32 [2, 2048], P('section')
All inputs are finite; a program needn't handle non-finite values.
Results may differ from a plain program's by a relative error of at most 0.001.
Values may be sent and summed in bfloat16 or wider, within the bound.
A program may use at most 128 MiB of HBM per device.

v0:
```python
import jax
import jax.numpy as jnp
from jax import lax
from jax.sharding import PartitionSpec as P

STEP = 10


beta_one = 0.9
beta_two = 0.95
learn_rate = 0.01
decay_rate = 0.1
small_eps = 1e-08
average_decay = 0.9


def adamw_update(weight, first, second, grad):
    first_new = beta_one * first + (1.0 - beta_one) * grad
    second_new = beta_two * second + (1.0 - beta_two) * grad * grad
    first_hat = first_new / (1.0 - beta_one**STEP)
    second_hat = second_new / (1.0 - beta_two**STEP)
    weight_new = weight - learn_rate * (
        first_hat / (jnp.sqrt(second_hat) + small_eps) + decay_rate * weight
    )
    return (weight_new, first_new, second_new)


def local(grads, gain_grads, master, moment1, moment2, average, gain_master, gain_m, gain_v):
    local_block = grads[0, 0, 0]
    width_rows, block_cols = local_block.shape
    shards = lax.axis_size("shard")
    pieces = lax.psum_scatter(
        local_block.T.astype(jnp.float32), "shard", scatter_dimension=0, tiled=True
    )
    local_squares = jnp.sum(pieces * pieces)
    group_size = lax.axis_size(("shard", "tensor"))
    gain_piece = lax.psum(gain_grads[0], ("shard", "tensor"))
    gain_weight, gain_first, gain_second = (gain_master, gain_m, gain_v)
    gain_squares = jnp.sum(gain_piece * gain_piece) / float(group_size)
    squares = lax.psum(local_squares + gain_squares, ("shard", "tensor", "section"))
    number = float(
        lax.axis_size("section") * lax.axis_size("tensor") * width_rows * block_cols
        + lax.axis_size("section") * width_rows
    )
    rms_value = jnp.sqrt(squares / number + 1e-06)
    clip = jnp.minimum(1.0, 1.0 / rms_value)
    new_master, new_m, new_v = adamw_update(
        master[0, 0], moment1[0, 0], moment2[0, 0], clip * pieces
    )
    gain_new, gain_first_new, gain_second_new = adamw_update(
        gain_weight, gain_first, gain_second, clip * gain_piece
    )
    avg_rows = width_rows // shards
    row_start = lax.axis_index("shard") * avg_rows
    piece = lax.all_gather(new_master, "shard", axis=0, tiled=True)
    weight_buf = piece.T.astype(jnp.bfloat16)
    own_rows = lax.dynamic_slice_in_dim(piece, row_start, avg_rows, 1).T
    new_average = average_decay * average[0, 0] + (1.0 - average_decay) * own_rows
    return (
        new_master[None, None],
        new_m[None, None],
        new_v[None, None],
        weight_buf[None, None],
        new_average[None, None],
        gain_new,
        gain_first_new,
        gain_second_new,
    )


def solution(mesh):
    placed = (
        P("section", "tensor", "shard", None, None),
        P("section", ("shard", "tensor"), None),
        P("section", "tensor", "shard", None),
        P("section", "tensor", "shard", None),
        P("section", "tensor", "shard", None),
        P("section", "tensor", "shard", None),
        P("section", None),
        P("section", None),
        P("section", None),
    )
    return jax.shard_map(
        local,
        mesh=mesh,
        in_specs=placed,
        out_specs=(
            P("section", "tensor", "shard", None),
            P("section", "tensor", "shard", None),
            P("section", "tensor", "shard", None),
            P("section", "tensor", None, None),
            P("section", "tensor", "shard", None),
            P("section", None),
            P("section", None),
            P("section", None),
        ),
        check_vma=False,
    )
```

profile of v0, /device:TPU:1, one launch (start us, length us, event | category | flops | bytes accessed | tf_op | source)
XLA Modules:
  0.0 341.6 jit_solution(4639558142823791613)
XLA Ops:
  7.2 0.0 reduce-scatter.2.cloned.1.call-start
  7.2 8.6 %copy.20 = bf16[1,1,1,2048,1536]{3,4,2,1,0:T(8,128)(2,1)} copy(bf16[1,1,1,2048,1536]{4,3,2,1,0:T(8,128)(2,1)} %param.9) | data formatting | bytes 12582912 | tf_op args[0]
  15.8 8.9 %convert_bitcast_fusion = f32[1536,2048]{1,0:T(8,128)} fusion(bf16[1,1,1,2048,1536]{3,4,2,1,0:T(8,128)(2,1)} %copy.20), kind=kLoop, calls=%fused_computation | loop fusion | flops 3145728 | bytes 18874368 | tf_op jit(solution)/shard_map/convert_element_type | solution.py:33
  24.7 0.0 reduce-scatter.2.cloned.1.call-update
  24.7 0.0 copy-start
  24.7 0.0 copy-start.4
  24.8 0.0 copy-start.5
  24.8 0.0 copy-start.6
  24.8 0.0 all-gather.2.cloned.1.call-start
  24.8 0.6 copy-done.7
  25.4 144.3 %psum.14 = f32[1,2048]{1,0:T(1,128)S(1)} all-reduce(f32[1,2048]{1,0:T(1,128)S(1)} %bitcast.45), channel_id=1, replica_groups=mesh['shard'=16,'tensor'=4,'section'=2] {'shard','tensor'}, use_global_device_ids=true, to_apply=%region_2.0 | all-reduce | flops 2048 | bytes 16384 | tf_op jit(solution)/shard_map/psum | solution.py:37
  169.7 0.6 multiply_reduce_fusion.1
  170.9 0.0 reduce-scatter.2.cloned.1.call-done
  171.0 1.9 multiply_reduce_fusion
  173.6 68.5 %psum.15 = f32[]{:T(128)} all-reduce(f32[]{:T(128)S(6)} %add.48), channel_id=1, replica_groups=mesh['shard'=16,'tensor'=4,'section'=2] {'shard','tensor','section'}, use_global_device_ids=true, to_apply=%region_4.0 | all-reduce | flops 1 | bytes 8 | tf_op jit(solution)/shard_map/psum | solution.py:40
  242.8 3.1 fusion.5
  245.9 0.0 all-gather.2.cloned.1.call-update
  246.0 0.3 copy.21
  246.3 0.7 multiply_subtract_fusion
  246.9 68.7 %all-gather.2.cloned.1.call-done = f32[1536,2048]{1,0:T(8,128)} async-done(((f32[96,2048]{1,0:T(8,128)}), f32[1536,2048]{1,0:T(8,128)}) %all-gather.2.cloned.1.call-update) | async-done | bytes 12582928 | tf_op jit(solution)/shard_map/all_gather | solution.py:55
  315.6 1.3 fusion.1
  316.8 1.1 copy.23
  318.0 8.2 %convert_bitcast_fusion.1 = bf16[1,1,2048,1536]{2,3,1,0:T(8,128)(2,1)} fusion(f32[1536,2048]{1,0:T(8,128)} %all-gather.2.cloned.1.call-done), kind=kLoop, calls=%fused_computation.1 | loop fusion | flops 3145728 | bytes 18874368 | tf_op jit(solution)/shard_map/broadcast_in_dim | solution.py:63
  326.2 8.6 %copy.22 = bf16[1,1,2048,1536]{3,2,1,0:T(8,128)(2,1)} copy(bf16[1,1,2048,1536]{2,3,1,0:T(8,128)(2,1)} %convert_bitcast_fusion.1) | data formatting | bytes 12582912
  (11 shorter events, 0.0 us)
Async XLA Ops:
  7.2 163.8 %reduce-scatter.2.cloned.1.call-start = ((), (), s32[]{:S(2)}) async-start(), calls=%async_computation.1 | async-start | bytes 13369344 | tf_op jit(solution)/shard_map/reduce_scatter | solution.py:32
  24.7 0.7 copy-start.7
  24.7 218.1 %copy-start.1 = (f32[1,1,96,2048]{3,2,1,0:T(8,128)S(1)}, f32[1,1,96,2048]{3,2,1,0:T(8,128)}, u32[]{:S(2)}) copy-start(f32[1,1,96,2048]{3,2,1,0:T(8,128)} %param.13) | copy-start | bytes 2359300
  24.7 218.1 %copy-start.2 = (f32[1,1,96,2048]{3,2,1,0:T(8,128)S(1)}, f32[1,1,96,2048]{3,2,1,0:T(8,128)}, u32[]{:S(2)}) copy-start(f32[1,1,96,2048]{3,2,1,0:T(8,128)} %param.12) | copy-start | bytes 2359300
  24.7 218.1 %copy-start.3 = (f32[1,1,96,2048]{3,2,1,0:T(8,128)S(1)}, f32[1,1,96,2048]{3,2,1,0:T(8,128)}, u32[]{:S(2)}) copy-start(f32[1,1,96,2048]{3,2,1,0:T(8,128)} %param.11) | copy-start | bytes 2359300
  24.7 221.2 %copy-start = (f32[1,1,128,1536]{3,2,1,0:T(8,128)S(1)}, f32[1,1,128,1536]{3,2,1,0:T(8,128)}, u32[]{:S(2)}) copy-start(f32[1,1,128,1536]{3,2,1,0:T(8,128)} %param.14) | copy-start | bytes 2359300
  24.7 221.5 %copy-start.4 = (f32[1,2048]{1,0:T(1,128)S(1)}, f32[1,2048]{1,0:T(1,128)}, u32[]{:S(2)}) copy-start(f32[1,2048]{1,0:T(1,128)} %param.15) | copy-start | bytes 24580
  24.8 221.5 %copy-start.5 = (f32[1,2048]{1,0:T(1,128)S(1)}, f32[1,2048]{1,0:T(1,128)}, u32[]{:S(2)}) copy-start(f32[1,2048]{1,0:T(1,128)} %param.16) | copy-start | bytes 24580
  24.8 221.5 %copy-start.6 = (f32[1,2048]{1,0:T(1,128)S(1)}, f32[1,2048]{1,0:T(1,128)}, u32[]{:S(2)}) copy-start(f32[1,2048]{1,0:T(1,128)} %param.17) | copy-start | bytes 24580
  24.8 290.8 %all-gather.2.cloned.1.call-start = ((), (), s32[]{:S(2)}) async-start(), calls=%async_computation.2 | async-start | bytes 13369344 | tf_op jit(solution)/shard_map/all_gather | solution.py:55
Sparse Core Ops, SparseCore 0:
  24.9 84.7 reduce-scatter.1
  246.1 69.4 all-gather.1
where the time goes:
time: 342 us
  blocking collectives  213 us (62%)
  waiting for transfers between devices  68.7 us (20%)
  other arithmetic  24.6 us (7%)
  local copies, waits for them, and re-layouts  19.2 us (6%)
  between operations  16.2 us (5%)
    psum x1, blocking collectives, local(): gain_piece = lax.psum(gain_grads[0], ('shard', 'tensor'))  144 us
    all_gather x1, waiting for transfers between devices, local(): piece = lax.all_gather(new_master, 'shard', axis=0, tiled=True)  68.7 us
    psum x1, blocking collectives, local(): lax.psum(local_squares + gain_squares, ('shard', 'tensor', 'section'))  68.5 us
    unnamed x20, local copies, waits for them, and re-layouts  19.2 us
    convert_element_type x1, other arithmetic, local(): local_block.T.astype(jnp.float32)  8.86 us
    broadcast_in_dim x1, other arithmetic, local(): weight_buf[None, None]  8.16 us
  transfers between devices with their start and end apart: 2, of which 1 were waited for; matrix products, arithmetic and copies ran while one was open for 0% of the time, Pallas kernels for 0%

commit v1 on v0

v1 whole, which is shorter than its diff:
```python
import functools

import jax
import jax.numpy as jnp
from jax import lax
from jax.experimental import pallas as pl
from jax.experimental.pallas import tpu as pltpu
from jax.sharding import PartitionSpec as P

STEP = 10

beta_one = 0.9
beta_two = 0.95
learn_rate = 0.01
decay_rate = 0.1
small_eps = 1e-08
average_decay = 0.9

MESH = pl.DeviceIdType.MESH
F32 = jnp.float32
BF16 = jnp.bfloat16
NX, NZ, NC = 2, 4, 2


def adamw_update(weight, first, second, grad):
    first_new = beta_one * first + (1.0 - beta_one) * grad
    second_new = beta_two * second + (1.0 - beta_two) * grad * grad
    first_hat = first_new / (1.0 - beta_one**STEP)
    second_hat = second_new / (1.0 - beta_two**STEP)
    weight_new = weight - learn_rate * (
        first_hat / (jnp.sqrt(second_hat) + small_eps) + decay_rate * weight
    )
    return (weight_new, first_new, second_new)


def kernel(dims, grads, gain_in, master, mom1, mom2, average, gmaster, gmom1, gmom2,
           o_master, o_m, o_v, o_w, o_avg, o_g, o_gm, o_gv,
           raw, acc, buf1, buf2, buf3, bufb1, bufb2, bufb3, state, wts, low, lowr, avg_in,
           n1, n2, g1, g2, lsem, ssem, rsem, lsend, gsem):
    D, BW, NS, NT = dims
    H = D // 2
    CH = BW // 16
    GR = 2 * CH
    PR = 2 * GR
    XR = NZ * GR
    TL = min(128, H)
    RA = 112 * GR // 192
    RB = GR - RA
    RH = RB // 2
    BH = (48 * RB) // 80
    LR = D // 16

    s = lax.axis_index("shard")
    t = lax.axis_index("tensor")
    sec = lax.axis_index("section")
    x = s // (NZ * NC)
    z = lax.rem(s // NC, NZ)
    c = lax.rem(s, NC)
    xo, co = 1 - x, 1 - c
    p = z // 2

    def shard_of(xx, zz, cc):
        return (xx * NZ + zz) * NC + cc

    zp, zm, zo = lax.rem(z + 1, NZ), lax.rem(z + 3, NZ), lax.rem(z + 2, NZ)
    zf = (2 * p) + 1 - (z - 2 * p)
    zof = lax.rem(zf + 2, NZ)
    to_xn = {"shard": shard_of(xo, z, c)}
    to_zp = {"shard": shard_of(x, zp, c)}
    to_zm = {"shard": shard_of(x, zm, c)}
    to_co = {"shard": shard_of(x, z, co)}

    count = [0]
    started = []

    def send(src, dst, dev):
        k = count[0]
        count[0] += 1
        cp = pltpu.make_async_remote_copy(
            src_ref=src, dst_ref=dst, send_sem=ssem.at[k], recv_sem=rsem.at[k],
            device_id=dev, device_id_type=MESH)
        cp.start()
        started.append(cp)
        return cp

    lcount = [0]

    def local(src, dst):
        k = lcount[0]
        lcount[0] += 1
        cp = pltpu.make_async_copy(src, dst, lsem.at[k])
        cp.start()
        return cp

    def G(xx, zz):
        return pl.multiple_of((xx * NZ + zz) * GR, GR)

    def pair_cols(xx, pp):
        return pl.multiple_of(xx * XR + pp * PR, PR)

    half = pl.multiple_of(c * H, H)
    ohalf = pl.multiple_of(co * H, H)

    order = [(xo, 1 - p), (x, 1 - p), (xo, p), (x, p)]

    own = [local(grads.at[pl.ds(half, H), pl.ds(pair_cols(*q), PR)],
                 raw.at[0, :, pl.ds(pair_cols(*q), PR)]) for q in order]
    c_own = pl.multiple_of(c * CH, CH)
    c_oth = pl.multiple_of(co * CH, CH)
    st_own = [local(ref.at[:, pl.ds(half, H)], state.at[i, pl.ds(c_own, CH), :])
              for i, ref in enumerate((master, mom1, mom2))]
    avg_cp = local(average, avg_in)

    barrier = pltpu.get_barrier_semaphore()
    peers = []
    for i in range(1, 16):
        peers.append({"shard": lax.rem(s + i, 16)})
    sides = []
    for dx in range(NX):
        for ds_ in range(NS):
            for dt in range(NT):
                if dx + ds_ + dt:
                    dev = {"shard": shard_of(lax.rem(x + dx, NX), z, c),
                           "tensor": lax.rem(t + dt, NT),
                           "section": lax.rem(sec + ds_, NS)}
                    sides.append((dx, ds_, dt, dev))
                    if ds_ + dt:
                        peers.append(dev)
    for dev in peers:
        pl.semaphore_signal(barrier, inc=1, device_id=dev, device_id_type=MESH)
    pl.semaphore_wait(barrier, len(peers))

    exch = []
    for q in order:
        cols = pl.ds(pair_cols(*q), PR)
        exch.append(send(grads.at[pl.ds(ohalf, H), cols], raw.at[1, :, cols], to_co))

    slot1 = z * NC + c
    gpeers = []
    for dz in range(NZ):
        for dc in range(NC):
            if dz + dc:
                gpeers.append({"shard": shard_of(x, lax.rem(z + dz, NZ), lax.rem(c + dc, NC))})
    g1[slot1] = gain_in[...]
    gain_cp = [send(gain_in, g1.at[slot1], dev) for dev in gpeers]

    st_oth = [send(ref.at[:, pl.ds(ohalf, H)], state.at[i, pl.ds(c_own, CH), :], to_co)
              for i, ref in enumerate((master, mom1, mom2))]

    def produce(q):
        base = pair_cols(*q)

        @pl.loop(0, PR // 128)
        def _(j):
            cols = pl.ds(pl.multiple_of(base + j * 128, 128), 128)
            for rb in range(H // TL):
                rows = slice(rb * TL, (rb + 1) * TL)
                tile = raw[0, rows, cols].astype(F32) + raw[1, rows, cols].astype(F32)
                acc[cols, rows] = tile.T

    def add(dst_row, buf, rows, block=8):
        @pl.loop(0, rows // block)
        def _(i):
            d = pl.ds(pl.multiple_of(dst_row + i * block, 8), block)
            acc[d, :] = acc[d, :] + buf[pl.ds(pl.multiple_of(i * block, 8), block), :]

    def a_of(xx, zz):
        return acc.at[pl.ds(G(xx, zz), RA), :]

    def b_of(xx, zz, lo=0, n=None):
        return acc.at[pl.ds(pl.multiple_of(G(xx, zz) + RA + lo, 8), RB if n is None else n), :]

    own[0].wait()
    exch[0].wait_recv()
    produce(order[0])
    s_a1m = send(a_of(xo, zo), buf1.at[1], to_zm)
    s_b1 = [send(b_of(xo, zo), bufb1.at[0], to_xn),
            send(b_of(xo, zof), bufb1.at[1], to_xn)]
    own[1].wait()
    exch[1].wait_recv()
    produce(order[1])
    s_a1p = send(a_of(x, zo), buf1.at[0], to_zp)
    own[2].wait()
    exch[2].wait_recv()
    produce(order[2])
    s_b1 += [send(b_of(xo, zf), bufb1.at[2], to_xn),
             send(b_of(xo, z), bufb1.at[3], to_xn)]
    own[3].wait()
    exch[3].wait_recv()
    produce(order[3])
    s_np = send(a_of(xo, zp), buf2.at[0], to_zp)
    s_nm = send(a_of(x, zm), buf2.at[1], to_zm)

    for cp in gain_cp:
        cp.wait_recv()
    gsum = g1[0]
    for i in range(1, NZ * NC):
        gsum = gsum + g1[i]
    slot2 = x * NT + t
    gsem[...] = gsum
    g2[slot2] = gsum
    gain_cp2 = []
    for dx, ds_, dt, dev in sides:
        if ds_ == 0:
            gain_cp2.append(send(gsem, g2.at[slot2], dev))

    s_b1[0].wait_recv()
    add(G(x, zo) + RA, bufb1.at[0], RB)
    s_a1m.wait_recv()
    add(G(xo, zm), buf1.at[1], RA)
    s_dm = send(a_of(xo, zm), buf2.at[2], to_zm)
    s_a1p.wait_recv()
    add(G(x, zp), buf1.at[0], RA)
    s_dp = send(a_of(x, zp), buf2.at[3], to_zp)
    s_b2p = send(b_of(x, zo, 0, RH), bufb2.at[0], to_zp)
    s_b2m = send(b_of(x, zo, RH, RH), bufb2.at[1], to_zm)

    s_b1[1].wait_recv()
    add(G(x, zof) + RA, bufb1.at[1], RB)
    s_b1[2].wait_recv()
    add(G(x, zf) + RA, bufb1.at[2], RB)
    s_b3np = send(b_of(x, zp, RH, RH), bufb3.at[0], to_zp)
    s_b3nm = send(b_of(x, zm, 0, RH), bufb3.at[1], to_zm)

    s_np.wait_recv()
    s_dm.wait_recv()

    @pl.loop(0, RA // 8)
    def _(i):
        d = pl.ds(pl.multiple_of(G(xo, z) + i * 8, 8), 8)
        e = pl.ds(pl.multiple_of(i * 8, 8), 8)
        acc[d, :] = acc[d, :] + buf2[0, e, :] + buf2[2, e, :]

    s_a3 = send(a_of(xo, z), buf3, to_xn)
    s_b2p.wait_recv()
    add(G(x, zp) + RA, bufb2.at[0], RH)
    s_b3dp = send(b_of(x, zp, 0, RH), bufb3.at[2], to_zp)
    s_b2m.wait_recv()
    add(G(x, zm) + RA + RH, bufb2.at[1], RH)
    s_b3dm = send(b_of(x, zm, RH, RH), bufb3.at[3], to_zm)

    s_nm.wait_recv()
    s_dp.wait_recv()

    @pl.loop(0, RA // 8)
    def _(i):
        d = pl.ds(pl.multiple_of(G(x, z) + i * 8, 8), 8)
        e = pl.ds(pl.multiple_of(i * 8, 8), 8)
        acc[d, :] = acc[d, :] + buf2[1, e, :] + buf2[3, e, :]

    s_b1[3].wait_recv()
    add(G(x, z) + RA, bufb1.at[3], RB)

    for cp in gain_cp2:
        cp.wait_recv()
    gain_total = g2[0]
    for i in range(1, NX * NT):
        gain_total = gain_total + g2[i]
    for cp in st_own:
        cp.wait()
    for cp in st_oth:
        cp.wait_recv()

    s_b3np.wait_recv()
    s_b3nm.wait_recv()
    s_b3dp.wait_recv()
    s_b3dm.wait_recv()

    zero = jnp.zeros((8, H), F32)

    def b_rows(lo, from_p, from_m, sq):
        def body(i, carry):
            d = pl.ds(pl.multiple_of(G(x, z) + RA + lo + i * 8, 8), 8)
            e = pl.ds(pl.multiple_of(i * 8, 8), 8)
            v = acc[d, :] + bufb3[from_p, e, :] + bufb3[from_m, e, :]
            acc[d, :] = v
            return carry + v * v
        return lax.fori_loop(0, RH // 8, body, sq)

    sq = b_rows(0, 2, 1, zero)
    sq = b_rows(RH, 0, 3, sq)

    s_a3.wait_recv()

    def a_body(i, carry):
        d = pl.ds(pl.multiple_of(G(x, z) + i * 8, 8), 8)
        e = pl.ds(pl.multiple_of(i * 8, 8), 8)
        v = acc[d, :] + buf3[e, :]
        acc[d, :] = v
        return carry + v * v

    sq = lax.fori_loop(0, RA // 8, a_body, sq)

    LN = min(128, H)
    gsq = gain_total * gain_total
    tile = sq[:, 0:LN]
    gtile = gsq[:, 0:LN]
    for i in range(1, H // LN):
        tile = tile + sq[:, i * LN:(i + 1) * LN]
    for i in range(1, D // LN):
        gtile = gtile + gsq[:, i * LN:(i + 1) * LN]
    tile = tile + gtile * (1.0 / (8 * 16 * NT))
    n1[NZ * NC] = tile
    norm_cp = [send(n1.at[NZ * NC], n1.at[slot1], dev) for dev in gpeers]
    n1[slot1] = tile
    for cp in norm_cp:
        cp.wait_recv()
    tile = n1[0]
    for i in range(1, NZ * NC):
        tile = tile + n1[i]
    slot3 = (x * NS + sec) * NT + t
    n_side = NX * NS * NT
    n2[n_side] = tile
    norm_cp2 = [send(n2.at[n_side], n2.at[slot3], dev) for _, _, _, dev in sides]
    n2[slot3] = tile
    for cp in norm_cp2:
        cp.wait_recv()
    tile = n2[0]
    for i in range(1, n_side):
        tile = tile + n2[i]
    squares = jnp.sum(jnp.sum(tile, axis=0, keepdims=True), axis=1, keepdims=True)
    number = float(NS * NT * D * BW + NS * D)
    rms = jnp.sqrt(squares / number + 1e-06)
    clip = jnp.minimum(1.0, 1.0 / rms)

    mine = G(x, z)

    def update(i, carry):
        e = pl.ds(pl.multiple_of(i * 16, 16), 16)
        d = pl.ds(pl.multiple_of(mine + i * 16, 16), 16)
        nw, nm, nv = adamw_update(state[0, e, :], state[1, e, :], state[2, e, :], clip * acc[d, :])
        state[0, e, :] = nw
        state[1, e, :] = nm
        state[2, e, :] = nv
        hi = nw.astype(BF16)
        wts[c, d, :] = hi
        low[e, :] = (nw - hi.astype(F32)).astype(BF16)
        return carry

    lax.fori_loop(0, GR // 16, update, 0)

    def w_at(h, xx, zz, lo, n):
        return wts.at[h, pl.ds(pl.multiple_of(G(xx, zz) + lo, 16), n), :]

    def relay(xx, zz, lo, n, dev):
        ref = w_at(c, xx, zz, lo, n)
        return send(ref, ref, dev)

    x_a = relay(x, z, 0, RA, to_xn)
    p_a1 = relay(x, z, 0, RA, to_zp)
    m_a1 = relay(x, z, 0, RA, to_zm)
    p_b = relay(x, z, RA, RB, to_zp)
    m_b = relay(x, z, RA, RB, to_zm)
    x_b = [relay(x, z, RA, RB, to_xn)]
    chip = [relay(x, z, 0, GR, to_co)]

    base = count[0]
    count[0] += NZ * NX
    low_cp = []
    for dz in range(NZ):
        for dc in range(NC):
            zz, cc = lax.rem(z + dz, NZ), lax.rem(c + dc, NC)
            src = low.at[:, pl.ds(pl.multiple_of((zz * NC + cc) * LR, LR), LR)]
            cp = pltpu.make_async_remote_copy(
                src_ref=src, dst_ref=lowr.at[pl.ds(mine, GR), :],
                send_sem=lsend.at[dz * NC + dc], recv_sem=rsem.at[base + dz * NX + x],
                device_id={"shard": shard_of(c, zz, cc)}, device_id_type=MESH)
            low_cp.append(cp)
            if dz + dc:
                cp.start()
            else:
                @pl.when(c == x)
                def _():
                    pltpu.make_async_copy(src, lowr.at[pl.ds(mine, GR), :], rsem.at[base + x]).start()

                @pl.when(c != x)
                def _():
                    cp.start()

    x_a.wait_recv()
    p_a2 = relay(xo, z, 0, RA, to_zp)
    m_a2 = relay(xo, z, 0, RA, to_zm)
    chip.append(relay(xo, z, 0, RA, to_co))
    p_a1.wait_recv()
    p_f1 = relay(x, zm, 0, RA, to_zp)
    chip.append(relay(x, zm, 0, RA, to_co))
    m_a1.wait_recv()
    chip.append(relay(x, zp, 0, RA, to_co))
    p_b.wait_recv()
    p_fb = relay(x, zm, RA, BH, to_zp)
    x_b.append(relay(x, zm, RA, RB, to_xn))
    chip.append(relay(x, zm, RA, RB, to_co))
    m_b.wait_recv()
    m_fb = relay(x, zp, RA + BH, RB - BH, to_zm)
    x_b.append(relay(x, zp, RA, RB, to_xn))
    chip.append(relay(x, zp, RA, RB, to_co))
    m_a2.wait_recv()
    m_f1 = relay(xo, zp, 0, RA, to_zm)
    chip.append(relay(xo, zp, 0, RA, to_co))
    p_a2.wait_recv()
    chip.append(relay(xo, zm, 0, RA, to_co))
    p_fb.wait_recv()
    m_fb.wait_recv()
    x_b.append(relay(x, zo, RA, RB, to_xn))
    chip.append(relay(x, zo, RA, RB, to_co))

    outs = (o_master, o_m, o_v)
    out_own = [local(state.at[i, pl.ds(c_own, CH), :], ref.at[:, pl.ds(half, H)])
               for i, ref in enumerate(outs)]
    out_oth = [send(state.at[i, pl.ds(c_oth, CH), :], ref.at[:, pl.ds(half, H)], to_co)
               for i, ref in enumerate(outs)]
    new_g, new_gm, new_gv = adamw_update(gmaster[...], gmom1[...], gmom2[...], clip * gain_total)
    o_g[...] = new_g
    o_gm[...] = new_gm
    o_gv[...] = new_gv

    x_b[0].wait_recv()
    chip.append(relay(xo, z, RA, RB, to_co))
    p_f1.wait_recv()
    chip.append(relay(x, zo, 0, RA, to_co))

    def emit(h, q):
        first = pair_cols(*q)

        @pl.loop(0, PR // 128)
        def _(j):
            cols = pl.ds(pl.multiple_of(first + j * 128, 128), 128)
            for rb in range(H // TL):
                o_w[pl.ds(pl.multiple_of(h * H + rb * TL, TL), TL), cols] = wts[h, cols, rb * TL:(rb + 1) * TL].T

    emit(c, (x, p))
    m_f1.wait_recv()
    chip.append(relay(xo, zo, 0, RA, to_co))
    emit(c, (x, 1 - p))
    x_b[1].wait_recv()
    chip.append(relay(xo, zm, RA, RB, to_co))
    x_b[2].wait_recv()
    chip.append(relay(xo, zp, RA, RB, to_co))
    x_b[3].wait_recv()
    chip.append(relay(xo, zo, RA, RB, to_co))
    emit(c, (xo, p))
    emit(c, (xo, 1 - p))
    for cp in chip:
        cp.wait_recv()
    for q in order:
        emit(co, q)
    for i in range(NZ * NX):
        pltpu.make_async_copy(lowr.at[pl.ds(0, GR), :], lowr.at[pl.ds(0, GR), :], rsem.at[base + i]).wait()
    avg_cp.wait()
    lanes = pl.ds(pl.multiple_of((z * NC + c) * LR, LR), LR)

    @pl.loop(0, BW // 128)
    def _(j):
        cols = pl.ds(pl.multiple_of(j * 128, 128), 128)
        nw = wts[x, cols, lanes].astype(F32) + lowr[cols, :].astype(F32)
        o_avg[:, cols] = average_decay * avg_in[:, cols] + (1.0 - average_decay) * nw.T

    for cp in out_own:
        cp.wait()
    for cp in out_oth:
        cp.wait_recv()
    for cp in started:
        cp.wait_send()
    for i, cp in enumerate(low_cp):
        if i:
            cp.wait_send()
        else:
            @pl.when(c != x)
            def _():
                cp.wait_send()


def local(dims, grads, gain_grads, master, moment1, moment2, average, gain_master, gain_m, gain_v):
    D, BW, NS, NT = dims
    H, CH = D // 2, BW // 16
    GR = 2 * CH
    RA = 112 * GR // 192
    RB = GR - RA
    LN = min(128, H)
    vm, sem = pltpu.VMEM, pltpu.SemaphoreType
    hbm = pl.BlockSpec(memory_space=pltpu.HBM)
    vmem = pl.BlockSpec(memory_space=pltpu.VMEM)
    shape = lambda sh, dt=F32: jax.ShapeDtypeStruct(sh, dt)
    outs = pl.pallas_call(
        functools.partial(kernel, dims),
        out_shape=(shape((CH, D)), shape((CH, D)), shape((CH, D)), shape((D, BW), BF16),
                   shape((D // 16, BW)), shape((1, D)), shape((1, D)), shape((1, D))),
        in_specs=[hbm, vmem, hbm, hbm, hbm, hbm, vmem, vmem, vmem],
        out_specs=[vmem] * 8,
        scratch_shapes=[
            vm((2, H, BW), BF16),
            vm((BW, H), F32),
            vm((2, RA, H), F32),
            vm((4, RA, H), F32),
            vm((RA, H), F32),
            vm((4, RB, H), F32),
            vm((2, RB // 2, H), F32),
            vm((4, RB // 2, H), F32),
            vm((3, GR, H), F32),
            vm((2, BW, H), BF16),
            vm((GR, H), BF16),
            vm((BW, D // 16), BF16),
            vm((D // 16, BW), F32),
            vm((9, 8, LN), F32),
            vm((NX * NS * NT + 1, 8, LN), F32),
            vm((8, 1, D), F32),
            vm((NX * NT, 1, D), F32),
            sem.DMA((16,)),
            sem.DMA((120,)),
            sem.DMA((120,)),
            sem.DMA((8,)),
            vm((1, D), F32),
        ],
        compiler_params=pltpu.CompilerParams(
            collective_id=0, has_side_effects=True, vmem_limit_bytes=48 * 2**20),
        name="adamw_step",
    )(grads[0, 0, 0], gain_grads[0], master[0, 0], moment1[0, 0], moment2[0, 0], average[0, 0],
      gain_master, gain_m, gain_v)
    new_master, new_m, new_v, weights, new_average, g, gm, gv = outs
    return (new_master[None, None], new_m[None, None], new_v[None, None], weights[None, None],
            new_average[None, None], g, gm, gv)


def solution(mesh):
    whole = P("section", "tensor", "shard", None)
    gains = P("section", None)

    def step(grads, *rest):
        dims = (grads.shape[3], grads.shape[4], mesh.shape["section"], mesh.shape["tensor"])
        return jax.shard_map(
            functools.partial(local, dims),
            mesh=mesh,
            in_specs=(P("section", "tensor", "shard", None, None), P("section", ("shard", "tensor"), None),
                      whole, whole, whole, whole, gains, gains, gains),
            out_specs=(whole, whole, whole, P("section", "tensor", None, None), whole, gains, gains, gains),
            check_vma=False,
        )(grads, *rest)

    return step
```

time: 342 us -> 124 us (0.36)
  blocking collectives: 213 us -> 0 us
  Pallas kernels: 0 us -> 105 us
  waiting for transfers between devices: 68.7 us -> 0 us
  other arithmetic: 24.6 us -> 0 us
  between operations: 16.2 us -> 0.66 us
    psum x2 -> x0, blocking collectives: 213 us -> none  [the longest x1 144 us: local(): gain_piece = lax.psum(gain_grads[0], ('shard', 'tensor'))]
    pallas_call x0 -> x1, Pallas kernels: none -> 105 us  [local(): pl.pallas_call(functools.partial(kernel, dims), out_shape=(shape((CH, D))...]
    all_gather x1 -> x0, waiting for transfers between devices: 68.7 us -> none  [local(): piece = lax.all_gather(new_master, 'shard', axis=0, tiled=True)]
    broadcast_in_dim x3 -> x0, other arithmetic: 12.6 us -> none  [the longest x1 8.16 us: local(): weight_buf[None, None]]
    convert_element_type x1 -> x0, other arithmetic: 8.86 us -> none  [local(): local_block.T.astype(jnp.float32)]
    unnamed x20 -> x22, local copies, waits for them, and re-layouts: 19.2 us -> 17.4 us
  transfers between devices with their start and end apart: 2 -> 0, of which waited for: 1 -> 0; matrix products, arithmetic and copies ran while one was open for 0% -> 0% of each run, Pallas kernels for 0% -> 0%
where the time goes in v1:
time: 124 us; the launch traced here: 123 us
  Pallas kernels  105 us (85%)
  local copies, waits for them, and re-layouts  17.4 us (14%)
    pallas_call x1, Pallas kernels, local(): pl.pallas_call(functools.partial(kernel, dims), out_shape=(shape((CH, D))...  105 us
    unnamed x22, local copies, waits for them, and re-layouts  17.4 us

profile of v1, /device:TPU:1, one launch (start us, length us, event | category | flops | bytes accessed | tf_op | source)
XLA Modules:
  0.0 123.1 jit_solution(2507746196783536778)
XLA Ops:
  0.6 0.0 copy-start
  0.6 1.1 copy-done
  1.8 0.0 copy-start.1
  1.8 1.1 copy-done.1
  2.9 0.0 copy-start.2
  2.9 1.1 copy-done.2
  4.0 0.0 copy-start.3
  4.0 0.7 copy-done.3
  4.7 0.0 copy-start.4
  4.7 0.7 copy-done.4
  5.4 0.0 copy-start.5
  5.4 0.7 copy-done.5
  6.1 0.0 copy-start.6
  6.1 0.7 copy-done.6
  6.8 105.0 %adamw_step.1 = (f32[96,2048]{1,0:T(8,128)S(1)}, f32[96,2048]{1,0:T(8,128)S(1)}, f32[96,2048]{1,0:T(8,128)S(1)}, bf16[2048,1536]{1,0:T(8,128)(2,1)}, f32[128,153...) custom-call(bf16[2048,1536]{1,0:T(8,128)(2,1)} %bitcast.19, ...), custom_call_target="tpu_custom_call" | custom-call | tf_op jit(solution)/shard_map/adamw_step/pallas_call | solution.py:484
  111.9 0.9 copy.25
  112.8 0.9 copy.26
  113.6 0.9 copy.27
  114.5 5.9 %copy.28 = bf16[1,1,2048,1536]{3,2,1,0:T(8,128)(2,1)} copy(bf16[1,1,2048,1536]{3,2,1,0:T(8,128)(2,1)} %bitcast.20) | data formatting | bytes 12582912
  120.4 0.9 copy.29
  121.3 0.6 copy.30
  121.9 0.6 copy.31
  122.5 0.6 copy.32
Async XLA Ops:
  0.6 1.1 copy-start
  1.8 1.1 copy-start.1
  2.9 1.1 copy-start.2
  4.0 0.7 copy-start.3
  4.7 0.7 copy-start.4
  5.4 0.7 copy-start.5
  6.1 0.7 copy-start.6

commit v2 on v1

--- a/solution.py
+++ b/solution.py
@@ -35,7 +35,7 @@
 
 def kernel(dims, grads, gain_in, master, mom1, mom2, average, gmaster, gmom1, gmom2,
            o_master, o_m, o_v, o_w, o_avg, o_g, o_gm, o_gv,
-           raw, acc, buf1, buf2, buf3, bufb1, bufb2, bufb3, state, wts, low, lowr, avg_in,
+           raw, acc, buf1, buf2, buf3, bufb1, bufb2, bufb3, state, wts, low, lowr, avg_in, gbuf,
            n1, n2, g1, g2, lsem, ssem, rsem, lsend, gsem):
     D, BW, NS, NT = dims
     H = D // 2
@@ -110,6 +110,7 @@
     st_own = [local(ref.at[:, pl.ds(half, H)], state.at[i, pl.ds(c_own, CH), :])
               for i, ref in enumerate((master, mom1, mom2))]
     avg_cp = local(average, avg_in)
+    gain_own = [local(ref, gbuf.at[i]) for i, ref in enumerate((gain_in, gmaster, gmom1, gmom2))]
 
     barrier = pltpu.get_barrier_semaphore()
     peers = []
@@ -141,8 +142,10 @@
         for dc in range(NC):
             if dz + dc:
                 gpeers.append({"shard": shard_of(x, lax.rem(z + dz, NZ), lax.rem(c + dc, NC))})
-    g1[slot1] = gain_in[...]
-    gain_cp = [send(gain_in, g1.at[slot1], dev) for dev in gpeers]
+    for cp in gain_own:
+        cp.wait()
+    g1[slot1] = gbuf[0]
+    gain_cp = [send(gbuf.at[0], g1.at[slot1], dev) for dev in gpeers]
 
     st_oth = [send(ref.at[:, pl.ds(ohalf, H)], state.at[i, pl.ds(c_own, CH), :], to_co)
               for i, ref in enumerate((master, mom1, mom2))]
@@ -337,8 +340,6 @@
         low[e, :] = (nw - hi.astype(F32)).astype(BF16)
         return carry
 
-    lax.fori_loop(0, GR // 16, update, 0)
-
     def w_at(h, xx, zz, lo, n):
         return wts.at[h, pl.ds(pl.multiple_of(G(xx, zz) + lo, 16), n), :]
 
@@ -346,13 +347,71 @@
         ref = w_at(c, xx, zz, lo, n)
         return send(ref, ref, dev)
 
+    lax.fori_loop(0, RA // 16, update, 0)
     x_a = relay(x, z, 0, RA, to_xn)
     p_a1 = relay(x, z, 0, RA, to_zp)
     m_a1 = relay(x, z, 0, RA, to_zm)
+    lax.fori_loop(RA // 16, GR // 16, update, 0)
     p_b = relay(x, z, RA, RB, to_zp)
     m_b = relay(x, z, RA, RB, to_zm)
     x_b = [relay(x, z, RA, RB, to_xn)]
-    chip = [relay(x, z, 0, GR, to_co)]
+
+    def on_chip(xx, zz, lo, n):
+        return relay(xx, zz, lo, n, to_co)
+
+    k_own = on_chip(x, z, 0, GR)
+
+    def emit(h, q):
+        first = pair_cols(*q)
+
+        @pl.loop(0, PR // 128)
+        def _(j):
+            cols = pl.ds(pl.multiple_of(first + j * 128, 128), 128)
+            for rb in range(H // TL):
+                o_w[pl.ds(pl.multiple_of(h * H + rb * TL, TL), TL), cols] = wts[h, cols, rb * TL:(rb + 1) * TL].T
+
+    outs = (o_master, o_m, o_v)
+    out_own = [local(state.at[i, pl.ds(c_own, CH), :], ref.at[:, pl.ds(half, H)])
+               for i, ref in enumerate(outs)]
+    new_g, new_gm, new_gv = adamw_update(gbuf[1], gbuf[2], gbuf[3], clip * gain_total)
+    o_g[...] = new_g
+    o_gm[...] = new_gm
+    o_gv[...] = new_gv
+
+    x_a.wait_recv()
+    p_a2 = relay(xo, z, 0, RA, to_zp)
+    m_a2 = relay(xo, z, 0, RA, to_zm)
+    k_xa = on_chip(xo, z, 0, RA)
+    p_a1.wait_recv()
+    k_ma = on_chip(x, zm, 0, RA)
+    m_a1.wait_recv()
+    k_pa = on_chip(x, zp, 0, RA)
+    p_b.wait_recv()
+    x_b.append(relay(x, zm, RA, RB, to_xn))
+    p_fb = relay(x, zm, RA, BH, to_zp)
+    k_mb = on_chip(x, zm, RA, RB)
+    m_b.wait_recv()
+    x_b.append(relay(x, zp, RA, RB, to_xn))
+    m_fb = relay(x, zp, RA + BH, RB - BH, to_zm)
+    k_pb = on_chip(x, zp, RA, RB)
+    p_f1 = relay(x, zm, 0, RA, to_zp)
+    x_b[0].wait_recv()
+    k_xb = on_chip(xo, z, RA, RB)
+    emit(c, (x, p))
+    m_a2.wait_recv()
+    m_f1 = relay(xo, zp, 0, RA, to_zm)
+    k_xpa = on_chip(xo, zp, 0, RA)
+    p_a2.wait_recv()
+    k_xma = on_chip(xo, zm, 0, RA)
+    out_oth = [send(state.at[i, pl.ds(c_oth, CH), :], ref.at[:, pl.ds(half, H)], to_co)
+               for i, ref in enumerate(outs)]
+    for cp in (k_own, k_ma, k_pa, k_mb, k_pb):
+        cp.wait_recv()
+    emit(co, (x, p))
+    p_fb.wait_recv()
+    m_fb.wait_recv()
+    x_b.append(relay(x, zo, RA, RB, to_xn))
+    k_ob = on_chip(x, zo, RA, RB)
 
     base = count[0]
     count[0] += NZ * NX
@@ -377,73 +436,28 @@
                 def _():
                     cp.start()
 
-    x_a.wait_recv()
-    p_a2 = relay(xo, z, 0, RA, to_zp)
-    m_a2 = relay(xo, z, 0, RA, to_zm)
-    chip.append(relay(xo, z, 0, RA, to_co))
-    p_a1.wait_recv()
-    p_f1 = relay(x, zm, 0, RA, to_zp)
-    chip.append(relay(x, zm, 0, RA, to_co))
-    m_a1.wait_recv()
-    chip.append(relay(x, zp, 0, RA, to_co))
-    p_b.wait_recv()
-    p_fb = relay(x, zm, RA, BH, to_zp)
-    x_b.append(relay(x, zm, RA, RB, to_xn))
-    chip.append(relay(x, zm, RA, RB, to_co))
-    m_b.wait_recv()
-    m_fb = relay(x, zp, RA + BH, RB - BH, to_zm)
-    x_b.append(relay(x, zp, RA, RB, to_xn))
-    chip.append(relay(x, zp, RA, RB, to_co))
-    m_a2.wait_recv()
-    m_f1 = relay(xo, zp, 0, RA, to_zm)
-    chip.append(relay(xo, zp, 0, RA, to_co))
-    p_a2.wait_recv()
-    chip.append(relay(xo, zm, 0, RA, to_co))
-    p_fb.wait_recv()
-    m_fb.wait_recv()
-    x_b.append(relay(x, zo, RA, RB, to_xn))
-    chip.append(relay(x, zo, RA, RB, to_co))
-
-    outs = (o_master, o_m, o_v)
-    out_own = [local(state.at[i, pl.ds(c_own, CH), :], ref.at[:, pl.ds(half, H)])
-               for i, ref in enumerate(outs)]
-    out_oth = [send(state.at[i, pl.ds(c_oth, CH), :], ref.at[:, pl.ds(half, H)], to_co)
-               for i, ref in enumerate(outs)]
-    new_g, new_gm, new_gv = adamw_update(gmaster[...], gmom1[...], gmom2[...], clip * gain_total)
-    o_g[...] = new_g
-    o_gm[...] = new_gm
-    o_gv[...] = new_gv
-
-    x_b[0].wait_recv()
-    chip.append(relay(xo, z, RA, RB, to_co))
+    x_b[1].wait_recv()
+    k_xmb = on_chip(xo, zm, RA, RB)
+    x_b[2].wait_recv()
+    k_xpb = on_chip(xo, zp, RA, RB)
+    emit(c, (xo, p))
+    for cp in (k_xa, k_xb, k_xpa, k_xma, k_xmb, k_xpb):
+        cp.wait_recv()
+    emit(co, (xo, p))
     p_f1.wait_recv()
-    chip.append(relay(x, zo, 0, RA, to_co))
-
-    def emit(h, q):
-        first = pair_cols(*q)
-
-        @pl.loop(0, PR // 128)
-        def _(j):
-            cols = pl.ds(pl.multiple_of(first + j * 128, 128), 128)
-            for rb in range(H // TL):
-                o_w[pl.ds(pl.multiple_of(h * H + rb * TL, TL), TL), cols] = wts[h, cols, rb * TL:(rb + 1) * TL].T
-
-    emit(c, (x, p))
+    k_oa = on_chip(x, zo, 0, RA)
     m_f1.wait_recv()
-    chip.append(relay(xo, zo, 0, RA, to_co))
+    k_xoa = on_chip(xo, zo, 0, RA)
+    x_b[3].wait_recv()
+    k_xob = on_chip(xo, zo, RA, RB)
     emit(c, (x, 1 - p))
-    x_b[1].wait_recv()
-    chip.append(relay(xo, zm, RA, RB, to_co))
-    x_b[2].wait_recv()
-    chip.append(relay(xo, zp, RA, RB, to_co))
-    x_b[3].wait_recv()
-    chip.append(relay(xo, zo, RA, RB, to_co))
-    emit(c, (xo, p))
+    for cp in (k_ob, k_oa):
+        cp.wait_recv()
+    emit(co, (x, 1 - p))
     emit(c, (xo, 1 - p))
-    for cp in chip:
-        cp.wait_recv()
-    for q in order:
-        emit(co, q)
+    for cp in (k_xoa, k_xob):
+        cp.wait_recv()
+    emit(co, (xo, 1 - p))
     for i in range(NZ * NX):
         pltpu.make_async_copy(lowr.at[pl.ds(0, GR), :], lowr.at[pl.ds(0, GR), :], rsem.at[base + i]).wait()
     avg_cp.wait()
@@ -468,6 +482,22 @@
             @pl.when(c != x)
             def _():
                 cp.wait_send()
+
+
+def store(*refs):
+    sems = refs[-1]
+    n = (len(refs) - 1) // 2
+    copies = []
+    for src, dst in zip(refs[:n], refs[n:2 * n]):
+        rows = src.shape[0]
+        parts = 8 if rows % 128 == 0 and rows > 1024 else 1
+        for i in range(parts):
+            r = pl.ds(i * (rows // parts), rows // parts)
+            copies.append(pltpu.make_async_copy(src.at[r, :], dst.at[r, :], sems.at[len(copies)]))
+    for cp in copies:
+        cp.start()
+    for cp in copies:
+        cp.wait()
 
 
 def local(dims, grads, gain_grads, master, moment1, moment2, average, gain_master, gain_m, gain_v):
@@ -485,7 +515,7 @@
         functools.partial(kernel, dims),
         out_shape=(shape((CH, D)), shape((CH, D)), shape((CH, D)), shape((D, BW), BF16),
                    shape((D // 16, BW)), shape((1, D)), shape((1, D)), shape((1, D))),
-        in_specs=[hbm, vmem, hbm, hbm, hbm, hbm, vmem, vmem, vmem],
+        in_specs=[hbm] * 9,
         out_specs=[vmem] * 8,
         scratch_shapes=[
             vm((2, H, BW), BF16),
@@ -501,21 +531,32 @@
             vm((GR, H), BF16),
             vm((BW, D // 16), BF16),
             vm((D // 16, BW), F32),
+            vm((4, 1, D), F32),
             vm((9, 8, LN), F32),
             vm((NX * NS * NT + 1, 8, LN), F32),
             vm((8, 1, D), F32),
             vm((NX * NT, 1, D), F32),
-            sem.DMA((16,)),
+            sem.DMA((24,)),
             sem.DMA((120,)),
             sem.DMA((120,)),
             sem.DMA((8,)),
             vm((1, D), F32),
         ],
         compiler_params=pltpu.CompilerParams(
-            collective_id=0, has_side_effects=True, vmem_limit_bytes=48 * 2**20),
+            collective_id=0, has_side_effects=True, vmem_limit_bytes=34 * 2**20),
         name="adamw_step",
-    )(grads[0, 0, 0], gain_grads[0], master[0, 0], moment1[0, 0], moment2[0, 0], average[0, 0],
-      gain_master, gain_m, gain_v)
+    )(*[pltpu.with_memory_space_constraint(a, pltpu.HBM) for a in (
+        grads[0, 0, 0], gain_grads[0], master[0, 0], moment1[0, 0], moment2[0, 0], average[0, 0],
+        gain_master, gain_m, gain_v)])
+    outs = pl.pallas_call(
+        store,
+        out_shape=[shape(o.shape, o.dtype) for o in outs],
+        in_specs=[pl.BlockSpec(memory_space=pl.ANY)] * 8,
+        out_specs=[pl.BlockSpec(memory_space=pl.ANY)] * 8,
+        scratch_shapes=[sem.DMA((16,))],
+        compiler_params=pltpu.CompilerParams(vmem_limit_bytes=2**20),
+        name="store",
+    )(*outs)
     new_master, new_m, new_v, weights, new_average, g, gm, gv = outs
     return (new_master[None, None], new_m[None, None], new_v[None, None], weights[None, None],
             new_average[None, None], g, gm, gv)

time: 124 us -> 98.9 us (0.80)
  local copies, waits for them, and re-layouts: 17.4 us -> 0 us
  Pallas kernels: 105 us -> 98.1 us
    unnamed x22 -> x0, local copies, waits for them, and re-layouts: 17.4 us -> none
    pallas_call x1, Pallas kernels: 105 us -> 94.4 us  [local(): pl.pallas_call(functools.partial(kernel, dims), out_shape=(shape((CH, D))...]
    pallas_call x0 -> x1, Pallas kernels: none -> 3.76 us  [local(): pl.pallas_call(store, out_shape=[shape(o.shape, o.dtype) for o in outs],...]
where the time goes in v2:
time: 98.9 us; the launch traced here: 98.8 us
  Pallas kernels  98.1 us (99%)
    pallas_call x1, Pallas kernels, local(): pl.pallas_call(functools.partial(kernel, dims), out_shape=(shape((CH, D))...  94.4 us
    pallas_call x1, Pallas kernels, local(): pl.pallas_call(store, out_shape=[shape(o.shape, o.dtype) for o in outs],...  3.76 us

profile of v2, /device:TPU:1, one launch (start us, length us, event | category | flops | bytes accessed | tf_op | source)
XLA Modules:
  0.0 98.8 jit_solution(6397074292768712772)
XLA Ops:
  0.6 94.4 %adamw_step.1 = (f32[96,2048]{1,0:T(8,128)S(1)}, f32[96,2048]{1,0:T(8,128)S(1)}, f32[96,2048]{1,0:T(8,128)S(1)}, bf16[2048,1536]{1,0:T(8,128)(2,1)S(1)}, f32[128...) custom-call(bf16[2048,1536]{1,0:T(8,128)(2,1)} %bitcast.11, ...), custom_call_target="tpu_custom_call" | custom-call | tf_op jit(solution)/shard_map/adamw_step/pallas_call | solution.py:514
  95.0 3.8 %store.1 = (f32[96,2048]{1,0:T(8,128)}, f32[96,2048]{1,0:T(8,128)}, f32[96,2048]{1,0:T(8,128)}, bf16[2048,1536]{1,0:T(8,128)(2,1)}, f32[128,1536]{1,0:T(8,128)},...) custom-call(f32[96,2048]{1,0:T(8,128)S(1)} %get-tuple-element.24.refs_0_, ...), custom_call_target="tpu_custom_call" | custom-call | tf_op jit(solution)/shard_map/store/pallas_call | solution.py:551

commit v3 on v2

--- a/solution.py
+++ b/solution.py
@@ -35,7 +35,7 @@
 
 def kernel(dims, grads, gain_in, master, mom1, mom2, average, gmaster, gmom1, gmom2,
            o_master, o_m, o_v, o_w, o_avg, o_g, o_gm, o_gv,
-           raw, acc, buf1, buf2, buf3, bufb1, bufb2, bufb3, state, wts, low, lowr, avg_in, gbuf,
+           raw, acc, buf1, buf2, buf3, bufb1, bufb2, bufb3, state, wts, low, lowr, avg_in, gbuf, pre,
            n1, n2, g1, g2, lsem, ssem, rsem, lsend, gsem):
     D, BW, NS, NT = dims
     H = D // 2
@@ -47,6 +47,7 @@
     RA = 112 * GR // 192
     RB = GR - RA
     RH = RB // 2
+    AH = RA // 2
     BH = (48 * RB) // 80
     LR = D // 16
 
@@ -103,8 +104,14 @@
 
     order = [(xo, 1 - p), (x, 1 - p), (xo, p), (x, p)]
 
+    odd = lax.rem(z, 2)
+    early = [(0, 0), (0, 1), (1, 0), (1, 1), (0, 2), (1, 2)]
+
     own = [local(grads.at[pl.ds(half, H), pl.ds(pair_cols(*q), PR)],
                  raw.at[0, :, pl.ds(pair_cols(*q), PR)]) for q in order]
+    early_cols = [pl.ds(pl.multiple_of(pair_cols(*order[u]) + (k + odd * (2 - 2 * k)) * 128, 128), 128)
+                  for u, k in early]
+    ahead = [local(grads.at[pl.ds(ohalf, H), cols], pre.at[i]) for i, cols in enumerate(early_cols)]
     c_own = pl.multiple_of(c * CH, CH)
     c_oth = pl.multiple_of(co * CH, CH)
     st_own = [local(ref.at[:, pl.ds(half, H)], state.at[i, pl.ds(c_own, CH), :])
@@ -132,7 +139,10 @@
     pl.semaphore_wait(barrier, len(peers))
 
     exch = []
-    for q in order:
+    for i, cols in enumerate(early_cols):
+        ahead[i].wait()
+        exch.append(send(pre.at[i], raw.at[1, :, cols], to_co))
+    for q in order[2:]:
         cols = pl.ds(pair_cols(*q), PR)
         exch.append(send(grads.at[pl.ds(ohalf, H), cols], raw.at[1, :, cols], to_co))
 
@@ -150,16 +160,18 @@
     st_oth = [send(ref.at[:, pl.ds(ohalf, H)], state.at[i, pl.ds(c_own, CH), :], to_co)
               for i, ref in enumerate((master, mom1, mom2))]
 
+    def produce_tile(cols):
+        for rb in range(H // TL):
+            rows = slice(rb * TL, (rb + 1) * TL)
+            tile = raw[0, rows, cols].astype(F32) + raw[1, rows, cols].astype(F32)
+            acc[cols, rows] = tile.T
+
     def produce(q):
         base = pair_cols(*q)
 
         @pl.loop(0, PR // 128)
         def _(j):
-            cols = pl.ds(pl.multiple_of(base + j * 128, 128), 128)
-            for rb in range(H // TL):
-                rows = slice(rb * TL, (rb + 1) * TL)
-                tile = raw[0, rows, cols].astype(F32) + raw[1, rows, cols].astype(F32)
-                acc[cols, rows] = tile.T
+            produce_tile(pl.ds(pl.multiple_of(base + j * 128, 128), 128))
 
     def add(dst_row, buf, rows, block=8):
         @pl.loop(0, rows // block)
@@ -167,32 +179,36 @@
             d = pl.ds(pl.multiple_of(dst_row + i * block, 8), block)
             acc[d, :] = acc[d, :] + buf[pl.ds(pl.multiple_of(i * block, 8), block), :]
 
-    def a_of(xx, zz):
-        return acc.at[pl.ds(G(xx, zz), RA), :]
+    def a_of(xx, zz, lo=0, n=None):
+        return acc.at[pl.ds(pl.multiple_of(G(xx, zz) + lo, 8), RA if n is None else n), :]
 
     def b_of(xx, zz, lo=0, n=None):
         return acc.at[pl.ds(pl.multiple_of(G(xx, zz) + RA + lo, 8), RB if n is None else n), :]
 
     own[0].wait()
-    exch[0].wait_recv()
-    produce(order[0])
-    s_a1m = send(a_of(xo, zo), buf1.at[1], to_zm)
-    s_b1 = [send(b_of(xo, zo), bufb1.at[0], to_xn),
-            send(b_of(xo, zof), bufb1.at[1], to_xn)]
     own[1].wait()
-    exch[1].wait_recv()
-    produce(order[1])
-    s_a1p = send(a_of(x, zo), buf1.at[0], to_zp)
+    for i, (u, k) in enumerate(early):
+        exch[i].wait_recv()
+        produce_tile(early_cols[i])
+        if i == 1:
+            s_b1 = [send(b_of(xo, zo), bufb1.at[0], to_xn)]
+            s_a1p = [send(a_of(xo, zo, AH, AH), buf1.at[0, 0], to_zp)]
+            s_a1m = [send(a_of(xo, zo, 0, AH), buf1.at[0, 1], to_zm)]
+        elif i == 3:
+            s_a1p.append(send(a_of(x, zo, AH, AH), buf1.at[1, 0], to_zp))
+            s_a1m.append(send(a_of(x, zo, 0, AH), buf1.at[1, 1], to_zm))
+        elif i == 4:
+            s_b1.append(send(b_of(xo, zof), bufb1.at[1], to_xn))
     own[2].wait()
-    exch[2].wait_recv()
+    exch[6].wait_recv()
     produce(order[2])
     s_b1 += [send(b_of(xo, zf), bufb1.at[2], to_xn),
              send(b_of(xo, z), bufb1.at[3], to_xn)]
     own[3].wait()
-    exch[3].wait_recv()
+    exch[7].wait_recv()
     produce(order[3])
-    s_np = send(a_of(xo, zp), buf2.at[0], to_zp)
-    s_nm = send(a_of(x, zm), buf2.at[1], to_zm)
+    s_np = [send(a_of(xo, zp, 0, AH), buf2.at[0, 0], to_zp)]
+    s_nm = [send(a_of(xo, zm, AH, AH), buf2.at[0, 1], to_zm)]
 
     for cp in gain_cp:
         cp.wait_recv()
@@ -209,12 +225,17 @@
 
     s_b1[0].wait_recv()
     add(G(x, zo) + RA, bufb1.at[0], RB)
-    s_a1m.wait_recv()
-    add(G(xo, zm), buf1.at[1], RA)
-    s_dm = send(a_of(xo, zm), buf2.at[2], to_zm)
-    s_a1p.wait_recv()
-    add(G(x, zp), buf1.at[0], RA)
-    s_dp = send(a_of(x, zp), buf2.at[3], to_zp)
+    s_dp, s_dm = [], []
+    for i, xx in enumerate((xo, x)):
+        s_a1p[i].wait_recv()
+        add(G(xx, zp) + AH, buf1.at[i, 0], AH)
+        s_dp.append(send(a_of(xx, zp, AH, AH), buf2.at[i, 2], to_zp))
+        s_a1m[i].wait_recv()
+        add(G(xx, zm), buf1.at[i, 1], AH)
+        s_dm.append(send(a_of(xx, zm, 0, AH), buf2.at[i, 3], to_zm))
+        if i == 0:
+            s_np.append(send(a_of(x, zp, 0, AH), buf2.at[1, 0], to_zp))
+            s_nm.append(send(a_of(x, zm, AH, AH), buf2.at[1, 1], to_zm))
     s_b2p = send(b_of(x, zo, 0, RH), bufb2.at[0], to_zp)
     s_b2m = send(b_of(x, zo, RH, RH), bufb2.at[1], to_zm)
 
@@ -225,16 +246,22 @@
     s_b3np = send(b_of(x, zp, RH, RH), bufb3.at[0], to_zp)
     s_b3nm = send(b_of(x, zm, 0, RH), bufb3.at[1], to_zm)
 
-    s_np.wait_recv()
-    s_dm.wait_recv()
-
-    @pl.loop(0, RA // 8)
-    def _(i):
-        d = pl.ds(pl.multiple_of(G(xo, z) + i * 8, 8), 8)
-        e = pl.ds(pl.multiple_of(i * 8, 8), 8)
-        acc[d, :] = acc[d, :] + buf2[0, e, :] + buf2[2, e, :]
-
-    s_a3 = send(a_of(xo, z), buf3, to_xn)
+    def meet(xx, i, lo, plain, summed):
+        @pl.loop(0, AH // 8)
+        def _(j):
+            d = pl.ds(pl.multiple_of(G(xx, z) + lo + j * 8, 8), 8)
+            e = pl.ds(pl.multiple_of(j * 8, 8), 8)
+            acc[d, :] = acc[d, :] + buf2[i, plain, e, :] + buf2[i, summed, e, :]
+
+    s_np[0].wait_recv()
+    s_nm[0].wait_recv()
+    s_a3 = []
+    s_dm[0].wait_recv()
+    meet(xo, 0, 0, 0, 3)
+    s_a3.append(send(a_of(xo, z, 0, AH), buf3.at[pl.ds(0, AH), :], to_xn))
+    s_dp[0].wait_recv()
+    meet(xo, 0, AH, 1, 2)
+    s_a3.append(send(a_of(xo, z, AH, AH), buf3.at[pl.ds(AH, AH), :], to_xn))
     s_b2p.wait_recv()
     add(G(x, zp) + RA, bufb2.at[0], RH)
     s_b3dp = send(b_of(x, zp, 0, RH), bufb3.at[2], to_zp)
@@ -242,14 +269,10 @@
     add(G(x, zm) + RA + RH, bufb2.at[1], RH)
     s_b3dm = send(b_of(x, zm, RH, RH), bufb3.at[3], to_zm)
 
-    s_nm.wait_recv()
-    s_dp.wait_recv()
-
-    @pl.loop(0, RA // 8)
-    def _(i):
-        d = pl.ds(pl.multiple_of(G(x, z) + i * 8, 8), 8)
-        e = pl.ds(pl.multiple_of(i * 8, 8), 8)
-        acc[d, :] = acc[d, :] + buf2[1, e, :] + buf2[3, e, :]
+    for cp in (s_np[1], s_nm[1], s_dm[1], s_dp[1]):
+        cp.wait_recv()
+    meet(x, 1, 0, 0, 3)
+    meet(x, 1, AH, 1, 2)
 
     s_b1[3].wait_recv()
     add(G(x, z) + RA, bufb1.at[3], RB)
@@ -283,8 +306,6 @@
     sq = b_rows(0, 2, 1, zero)
     sq = b_rows(RH, 0, 3, sq)
 
-    s_a3.wait_recv()
-
     def a_body(i, carry):
         d = pl.ds(pl.multiple_of(G(x, z) + i * 8, 8), 8)
         e = pl.ds(pl.multiple_of(i * 8, 8), 8)
@@ -292,7 +313,9 @@
         acc[d, :] = v
         return carry + v * v
 
-    sq = lax.fori_loop(0, RA // 8, a_body, sq)
+    for i, cp in enumerate(s_a3):
+        cp.wait_recv()
+        sq = lax.fori_loop(i * AH // 8, (i + 1) * AH // 8, a_body, sq)
 
     LN = min(128, H)
     gsq = gain_total * gain_total
@@ -347,10 +370,12 @@
         ref = w_at(c, xx, zz, lo, n)
         return send(ref, ref, dev)
 
-    lax.fori_loop(0, RA // 16, update, 0)
-    x_a = relay(x, z, 0, RA, to_xn)
-    p_a1 = relay(x, z, 0, RA, to_zp)
-    m_a1 = relay(x, z, 0, RA, to_zm)
+    x_a, p_a1, m_a1 = [], [], []
+    for lo, n in ((0, 48), (48, RA - 48)):
+        lax.fori_loop(lo // 16, (lo + n) // 16, update, 0)
+        x_a.append(relay(x, z, lo, n, to_xn))
+        p_a1.append(relay(x, z, lo, n, to_zp))
+        m_a1.append(relay(x, z, lo, n, to_zm))
     lax.fori_loop(RA // 16, GR // 16, update, 0)
     p_b = relay(x, z, RA, RB, to_zp)
     m_b = relay(x, z, RA, RB, to_zm)
@@ -378,13 +403,16 @@
     o_gm[...] = new_gm
     o_gv[...] = new_gv
 
-    x_a.wait_recv()
+    for cp in x_a:
+        cp.wait_recv()
     p_a2 = relay(xo, z, 0, RA, to_zp)
     m_a2 = relay(xo, z, 0, RA, to_zm)
     k_xa = on_chip(xo, z, 0, RA)
-    p_a1.wait_recv()
+    for cp in p_a1:
+        cp.wait_recv()
     k_ma = on_chip(x, zm, 0, RA)
-    m_a1.wait_recv()
+    for cp in m_a1:
+        cp.wait_recv()
     k_pa = on_chip(x, zp, 0, RA)
     p_b.wait_recv()
     x_b.append(relay(x, zm, RA, RB, to_xn))
@@ -416,7 +444,7 @@
     base = count[0]
     count[0] += NZ * NX
     low_cp = []
-    for dz in range(NZ):
+    for dz in (0, 1, 3, 2):
         for dc in range(NC):
             zz, cc = lax.rem(z + dz, NZ), lax.rem(c + dc, NC)
             src = low.at[:, pl.ds(pl.multiple_of((zz * NC + cc) * LR, LR), LR)]
@@ -458,16 +486,20 @@
     for cp in (k_xoa, k_xob):
         cp.wait_recv()
     emit(co, (xo, 1 - p))
-    for i in range(NZ * NX):
-        pltpu.make_async_copy(lowr.at[pl.ds(0, GR), :], lowr.at[pl.ds(0, GR), :], rsem.at[base + i]).wait()
     avg_cp.wait()
     lanes = pl.ds(pl.multiple_of((z * NC + c) * LR, LR), LR)
-
-    @pl.loop(0, BW // 128)
-    def _(j):
-        cols = pl.ds(pl.multiple_of(j * 128, 128), 128)
-        nw = wts[x, cols, lanes].astype(F32) + lowr[cols, :].astype(F32)
-        o_avg[:, cols] = average_decay * avg_in[:, cols] + (1.0 - average_decay) * nw.T
+    some = lowr.at[pl.ds(0, GR), :]
+    for pp, shifts in ((p, (0, lax.rem(z - zf + NZ, NZ))), (1 - p, (2, lax.rem(z - zof + NZ, NZ)))):
+        for xx in (x, xo):
+            for dz in shifts:
+                pltpu.make_async_copy(some, some, rsem.at[base + dz * NX + xx]).wait()
+            first = pair_cols(xx, pp)
+
+            @pl.loop(0, PR // 128)
+            def _(j):
+                cols = pl.ds(pl.multiple_of(first + j * 128, 128), 128)
+                nw = wts[x, cols, lanes].astype(F32) + lowr[cols, :].astype(F32)
+                o_avg[:, cols] = average_decay * avg_in[:, cols] + (1.0 - average_decay) * nw.T
 
     for cp in out_own:
         cp.wait()
@@ -490,7 +522,7 @@
     copies = []
     for src, dst in zip(refs[:n], refs[n:2 * n]):
         rows = src.shape[0]
-        parts = 8 if rows % 128 == 0 and rows > 1024 else 1
+        parts = 8 if rows > 1024 else 1
         for i in range(parts):
             r = pl.ds(i * (rows // parts), rows // parts)
             copies.append(pltpu.make_async_copy(src.at[r, :], dst.at[r, :], sems.at[len(copies)]))
@@ -520,8 +552,8 @@
         scratch_shapes=[
             vm((2, H, BW), BF16),
             vm((BW, H), F32),
-            vm((2, RA, H), F32),
-            vm((4, RA, H), F32),
+            vm((2, 2, RA // 2, H), F32),
+            vm((2, 4, RA // 2, H), F32),
             vm((RA, H), F32),
             vm((4, RB, H), F32),
             vm((2, RB // 2, H), F32),
@@ -532,18 +564,19 @@
             vm((BW, D // 16), BF16),
             vm((D // 16, BW), F32),
             vm((4, 1, D), F32),
+            vm((6, H, 128), BF16),
             vm((9, 8, LN), F32),
             vm((NX * NS * NT + 1, 8, LN), F32),
             vm((8, 1, D), F32),
             vm((NX * NT, 1, D), F32),
-            sem.DMA((24,)),
+            sem.DMA((32,)),
             sem.DMA((120,)),
             sem.DMA((120,)),
             sem.DMA((8,)),
             vm((1, D), F32),
         ],
         compiler_params=pltpu.CompilerParams(
-            collective_id=0, has_side_effects=True, vmem_limit_bytes=34 * 2**20),
+            collective_id=0, has_side_effects=True, vmem_limit_bytes=36 * 2**20),
         name="adamw_step",
     )(*[pltpu.with_memory_space_constraint(a, pltpu.HBM) for a in (
         grads[0, 0, 0], gain_grads[0], master[0, 0], moment1[0, 0], moment2[0, 0], average[0, 0],
@@ -553,7 +586,7 @@
         out_shape=[shape(o.shape, o.dtype) for o in outs],
         in_specs=[pl.BlockSpec(memory_space=pl.ANY)] * 8,
         out_specs=[pl.BlockSpec(memory_space=pl.ANY)] * 8,
-        scratch_shapes=[sem.DMA((16,))],
+        scratch_shapes=[sem.DMA((32,))],
         compiler_params=pltpu.CompilerParams(vmem_limit_bytes=2**20),
         name="store",
     )(*outs)

time: 98.9 us -> 96.3 us (0.974)
  Pallas kernels: 98.1 us -> 95.5 us
    pallas_call x1, Pallas kernels: 94.4 us -> 91.6 us  [local(): pl.pallas_call(functools.partial(kernel, dims), out_shape=(shape((CH, D))...]
where the time goes in v3:
time: 96.3 us; the launch traced here: 96.2 us
  Pallas kernels  95.5 us (99%)
    pallas_call x1, Pallas kernels, local(): pl.pallas_call(functools.partial(kernel, dims), out_shape=(shape((CH, D))...  91.6 us
    pallas_call x1, Pallas kernels, local(): pl.pallas_call(store, out_shape=[shape(o.shape, o.dtype) for o in outs],...  3.91 us

profile of v3, /device:TPU:1, one launch (start us, length us, event | category | flops | bytes accessed | tf_op | source)
XLA Modules:
  0.0 96.2 jit_solution(12600968963236616972)
XLA Ops:
  0.6 91.6 %adamw_step.1 = (f32[96,2048]{1,0:T(8,128)S(1)}, f32[96,2048]{1,0:T(8,128)S(1)}, f32[96,2048]{1,0:T(8,128)S(1)}, bf16[2048,1536]{1,0:T(8,128)(2,1)S(1)}, f32[128...) custom-call(bf16[2048,1536]{1,0:T(8,128)(2,1)} %bitcast.11, ...), custom_call_target="tpu_custom_call" | custom-call | tf_op jit(solution)/shard_map/adamw_step/pallas_call | solution.py:546
  92.3 3.9 %store.1 = (f32[96,2048]{1,0:T(8,128)}, f32[96,2048]{1,0:T(8,128)}, f32[96,2048]{1,0:T(8,128)}, bf16[2048,1536]{1,0:T(8,128)(2,1)}, f32[128,1536]{1,0:T(8,128)},...) custom-call(f32[96,2048]{1,0:T(8,128)S(1)} %get-tuple-element.24.refs_0_, ...), custom_call_target="tpu_custom_call" | custom-call | tf_op jit(solution)/shard_map/store/pallas_call | solution.py:584
